TPU v7x, 128 devices: a whole 4x4x4 slice. The times are simulated.
128 devices in a mesh: shard: 16 (over y, z), tensor: 4 (over x), section: 2 (over core).
Axes of the slice: x: 4, y: 4, z: 4, core: 2. Of those that a mesh axis runs over, the one named last changes fastest.
Arguments:
- attention_grads: float32 [16, 4, 768, 768], P('shard', 'section', 'tensor'), may hold values from -48 to 48
- feedforward_grads: float32 [16, 2, 3072, 768], P('shard', 'section', 'tensor'), may hold values from -48 to 48
- attention_errors: float32 [16, 4, 768, 768], P('shard', 'section', 'tensor'), may hold values from -3 to 3
- feedforward_errors: float32 [16, 2, 3072, 768], P('shard', 'section', 'tensor'), may hold values from -3 to 3
- attention_factor: float32 [4, 768, 32], P('section'), may hold values from -0.21875 to 0.21875
- feedforward_factor: float32 [2, 768, 32], P('section'), may hold values from -0.21875 to 0.21875
- attention_momentum: float32 [4, 768, 768], P('section', 'tensor', 'shard'), may hold values from -3 to 3
- feedforward_momentum: float32 [2, 3072, 768], P('section', 'tensor', 'shard'), may hold values from -3 to 3
- attention_master: float32 [4, 768, 768], P('section', 'tensor', 'shard'), may hold values from -3 to 3
- feedforward_master: float32 [2, 3072, 768], P('section', 'tensor', 'shard'), may hold values from -3 to 3
- gain_grads: float32 [16, 2, 768], P('shard', 'section', 'tensor'), may hold values from -6 to 6
- bias_grads: float32 [16, 12, 32], P('shard', 'tensor'), may hold values from -6 to 6
- gain_momentum: float32 [2, 768], P('section', 'tensor'), may hold values from -3 to 3
- gain_weight: float32 [2, 768], P('section', 'tensor'), may hold values from 0.5 to 1.5
- bias_momentum: float32 [12, 32], P('tensor'), may hold values from -3 to 3
- bias_weight: float32 [12, 32], P('tensor'), may hold values from -4 to 4
Outputs:
- attention_errors_new: float32 [16, 4, 768, 768], P('shard', 'section', 'tensor')
- feedforward_errors_new: float32 [16, 2, 3072, 768], P('shard', 'section', 'tensor')
- attention_factor_new: float32 [4, 768, 32], P('section')
- feedforward_factor_new: float32 [2, 768, 32], P('section')
- attention_momentum_new: float32 [4, 768, 768], P('section', 'tensor', 'shard')
- feedforward_momentum_new: float32 [2, 3072, 768], P('section', 'tensor', 'shard')
- attention_master_new: float32 [4, 768, 768], P('section', 'tensor', 'shard')
- feedforward_master_new: float32 [2, 3072, 768], P('section', 'tensor', 'shard')
- attention_fresh: bfloat16 [4, 768, 768], P('section', 'tensor')
- feedforward_fresh: bfloat16 [2, 3072, 768], P('section', 'tensor')
- gain_momentum_new: float32 [2, 768], P('section', 'tensor')
- gain_weight_new: float32 [2, 768], P('section', 'tensor')
- bias_momentum_new: float32 [12, 32], P('tensor')
- bias_weight_new: float32 [12, 32], P('tensor')
All inputs are finite; a program needn't handle non-finite values.
Results may differ from a plain program's by a relative error of at most 0.0004.
Values may be sent and summed in bfloat16 or wider, within the bound.
A program may use at most 64 MiB of HBM per device.

v0:
```python
import jax
import jax.numpy as jnp
from jax import lax
from jax.sharding import PartitionSpec as P

NS_STEPS = 5
exact_mode = lax.Precision.HIGHEST
learn_rate = 0.05
decay_rate = 0.9


def inverse_root(gram_matrix):
    identity = jnp.broadcast_to(
        jnp.eye(gram_matrix.shape[-1], dtype=jnp.float32), gram_matrix.shape
    )
    frob_scale = jnp.sqrt(jnp.sum(gram_matrix * gram_matrix, axis=(-2, -1), keepdims=True)) + 1e-06
    converge = gram_matrix / frob_scale
    inverse = identity
    for turn_index in range(NS_STEPS):
        middle = 0.5 * (3.0 * identity - jnp.matmul(inverse, converge, precision=exact_mode))
        converge, inverse = (
            jnp.matmul(converge, middle, precision=exact_mode),
            jnp.matmul(middle, inverse, precision=exact_mode),
        )
    return inverse / jnp.sqrt(frob_scale)


def left_terms(merged, factor):
    return jnp.einsum("rmij,mjk->mik", merged, factor, precision=exact_mode)


def row_gram(matrix):
    return jnp.einsum("mik,mil->mkl", matrix, matrix, precision=exact_mode)


def right_terms(merged, ortho):
    return jnp.einsum("rmij,mik->mjk", merged, ortho, precision=exact_mode)


def per_device(
    attention_grads,
    feedforward_grads,
    attention_errors,
    feedforward_errors,
    attention_factor,
    feedforward_factor,
    attention_momentum,
    feedforward_momentum,
    attention_master,
    feedforward_master,
    gain_grads,
    bias_grads,
    gain_momentum,
    gain_weight,
    bias_momentum,
    bias_weight,
):
    replicas = lax.axis_size("shard")
    column_width = attention_master.shape[2]
    column_start = lax.axis_index("shard") * column_width
    attention_base = attention_master - learn_rate * decay_rate * attention_momentum
    feedforward_base = feedforward_master - learn_rate * decay_rate * feedforward_momentum
    attention_merged = attention_grads + attention_errors
    feedforward_merged = feedforward_grads + feedforward_errors
    attention_part = left_terms(attention_merged, attention_factor)
    feedforward_part = left_terms(feedforward_merged, feedforward_factor)
    attention_power, feedforward_power = lax.psum((attention_part, feedforward_part), "shard")
    attention_gram, feedforward_gram = lax.psum(
        (row_gram(attention_power), row_gram(feedforward_power)), "tensor"
    )
    attention_ortho = jnp.matmul(
        attention_power, inverse_root(attention_gram), precision=exact_mode
    )
    feedforward_ortho = jnp.matmul(
        feedforward_power, inverse_root(feedforward_gram), precision=exact_mode
    )
    attention_back, feedforward_back = lax.psum(
        (
            right_terms(attention_merged, attention_ortho),
            right_terms(feedforward_merged, feedforward_ortho),
        ),
        ("shard", "tensor"),
    )
    attention_back = attention_back / replicas
    feedforward_back = feedforward_back / replicas
    attention_approx = jnp.einsum(
        "mik,mjk->mij", attention_ortho, attention_back, precision=exact_mode
    )
    feedforward_approx = jnp.einsum(
        "mik,mjk->mij", feedforward_ortho, feedforward_back, precision=exact_mode
    )
    attention_errors_new = attention_merged - attention_approx[None]
    feedforward_errors_new = feedforward_merged - feedforward_approx[None]
    attention_factor_new = jnp.matmul(
        attention_back, inverse_root(row_gram(attention_back)), precision=exact_mode
    )
    feedforward_factor_new = jnp.matmul(
        feedforward_back, inverse_root(row_gram(feedforward_back)), precision=exact_mode
    )
    attention_slice = lax.dynamic_slice_in_dim(attention_approx, column_start, column_width, 2)
    feedforward_slice = lax.dynamic_slice_in_dim(feedforward_approx, column_start, column_width, 2)
    attention_momentum_new = decay_rate * attention_momentum + attention_slice
    feedforward_momentum_new = decay_rate * feedforward_momentum + feedforward_slice
    attention_master_new = attention_base - learn_rate * attention_slice
    feedforward_master_new = feedforward_base - learn_rate * feedforward_slice
    attention_fresh, feedforward_fresh = (
        lax.all_gather(attention_master_new.astype(jnp.bfloat16), "shard", axis=2, tiled=True),
        lax.all_gather(feedforward_master_new.astype(jnp.bfloat16), "shard", axis=2, tiled=True),
    )
    gain_total, bias_total = lax.psum((gain_grads[0], bias_grads[0]), "shard")
    gain_momentum_new = decay_rate * gain_momentum + gain_total / replicas
    gain_weight_new = gain_weight - learn_rate * gain_momentum_new
    bias_momentum_new = decay_rate * bias_momentum + bias_total / replicas
    bias_weight_new = bias_weight - learn_rate * bias_momentum_new
    return (
        attention_errors_new,
        feedforward_errors_new,
        attention_factor_new,
        feedforward_factor_new,
        attention_momentum_new,
        feedforward_momentum_new,
        attention_master_new,
        feedforward_master_new,
        attention_fresh,
        feedforward_fresh,
        gain_momentum_new,
        gain_weight_new,
        bias_momentum_new,
        bias_weight_new,
    )


def solution(mesh):
    placed = (
        P("shard", "section", "tensor", None),
        P("shard", "section", "tensor", None),
        P("shard", "section", "tensor", None),
        P("shard", "section", "tensor", None),
        P("section", None, None),
        P("section", None, None),
        P("section", "tensor", "shard"),
        P("section", "tensor", "shard"),
        P("section", "tensor", "shard"),
        P("section", "tensor", "shard"),
        P("shard", "section", "tensor"),
        P("shard", "tensor", None),
        P("section", "tensor"),
        P("section", "tensor"),
        P("tensor", None),
        P("tensor", None),
    )
    return jax.shard_map(
        per_device,
        mesh=mesh,
        in_specs=placed,
        out_specs=(
            P("shard", "section", "tensor", None),
            P("shard", "section", "tensor", None),
            P("section", None, None),
            P("section", None, None),
            P("section", "tensor", "shard"),
            P("section", "tensor", "shard"),
            P("section", "tensor", "shard"),
            P("section", "tensor", "shard"),
            P("section", "tensor", None),
            P("section", "tensor", None),
            P("section", "tensor"),
            P("section", "tensor"),
            P("tensor", None),
            P("tensor", None),
        ),
        check_vma=False,
    )
```

profile of v0, /device:TPU:0, one launch (start us, length us, event | category | flops | bytes accessed | tf_op | source)
XLA Modules:
  0.0 321.8 jit_solution(5114528691584657770)
XLA Ops:
  7.3 3.2 copy.39
  10.5 2.0 copy.40
  12.4 2.7 add.70
  15.1 2.2 fusion.2
  17.4 1.8 add.68
  19.2 1.0 copy-done.1
  20.2 1.2 fusion.6
  21.5 76.9 %all-reduce.1 = (f32[2,192,32]{1,2,0:T(8,128)S(1)}, f32[1,192]{1,0:T(1,128)S(1)}, f32[3,32]{1,0:T(4,128)S(1)}) all-reduce(f32[2,192,32]{1,2,0:T(8,128)S(1)} %fusion.6, f32[1,192]{1,0:T(1,128)S(1)} %bitcast.162, f32[3,32]{1,0:T(4,128)S(1)} %bitcast.161), channel_id=1, replica_groups=mesh['shard'=16,'tensor'=4,'section'=2] {'shard'}, use_global_device_ids=true, to_apply=%region_0.0 | all-reduce | flops 12576 | bytes 100608 | tf_op jit(solution)/shard_map/psum | solution.py:67
  98.4 0.2 fusion.78
  98.6 3.7 %all-reduce.6.cloned.1.call-done = f32[768,32]{0,1:T(8,128)} async-done(((f32[768,32]{0,1:T(8,128)}), f32[768,32]{0,1:T(8,128)}) %all-reduce.6.cloned.1.call-update) | async-done | bytes 98320 | tf_op jit(solution)/shard_map/psum | solution.py:67
  102.3 1.3 convolution_bitcast_fusion.1
  103.6 17.4 %all-reduce.2 = (f32[2,32,32]{2,1,0:T(8,128)S(1)}, f32[1,32,32]{2,1,0:T(8,128)S(1)}) all-reduce(f32[2,32,32]{2,1,0:T(8,128)S(1)} %fusion.78, f32[1,32,32]{2,1,0:T(8,128)S(1)} %convolution_bitcast_fusion.1), channel_id=1, replica_groups=mesh['shard'=16,'tensor'=4,'section'=2] {'tensor'}, use_global_device_ids=true, to_apply=%region_1.0 | all-reduce | flops 3072 | bytes 24576 | tf_op jit(solution)/shard_map/psum | solution.py:68
  120.9 0.6 multiply_reduce_fusion.3
  123.1 0.2 fusion.28
  123.6 0.2 fusion.27
  124.2 0.2 fusion.20
  124.5 0.2 fusion.66
  124.9 0.2 fusion.19
  125.2 0.2 fusion.79
  125.4 0.2 fusion.18
  125.6 0.2 fusion.82
  125.9 0.2 fusion.17
  126.1 0.2 fusion.84
  126.2 0.2 fusion.83
  126.7 0.3 fusion.92
  127.1 2.8 fusion.8
  129.9 0.2 fusion.16
  130.1 0.2 convolution_divide_fusion.1
  130.3 0.2 fusion.85
  130.5 1.4 fusion.4
  132.0 0.2 all-gather.2.cloned.1.call-start
  132.2 0.6 multiply_subtract_fusion.2
  133.1 0.6 multiply_subtract_fusion.1
  133.7 121.8 %all-reduce.8.cloned.1.call-done = (f32[2,768,32]{1,2,0:T(8,128)}, f32[1,768,32]{1,2,0:T(8,128)}) async-done(((f32[2,768,32]{1,2,0:T(8,128)}, f32[1,768,32]{1,2,0:T(8,128)}), (f32[2,768,32]{1,2,0:T(8,128)}, f32[1,768,32]{1,2,0:T(8,128)})) %all-reduce.8.cloned.1.call-update) | async-done | bytes 294928 | tf_op jit(solution)/shard_map/psum | solution.py:77
  255.5 1.8 multiply_reduce_fusion.2
  258.8 0.2 fusion.23
  259.3 0.2 fusion.22
  259.8 1.4 multiply_reduce_fusion
  261.3 0.6 fusion.75
  261.8 0.2 fusion.15
  262.1 0.2 fusion.67
  262.5 0.2 fusion.14
  262.7 0.8 fusion.94
  263.4 0.8 fusion.93
  264.2 4.5 %bitcast_subtract_fusion = (f32[1,1,768,768]{2,3,1,0:T(8,128)}, f32[768,768]{0,1:T(8,128)S(1)}) fusion(f32[1,1,768,768]{2,3,1,0:T(8,128)S(1)} %add.70, f32[768,32]{0,1:T(8,128)S(1)} %fusion.92, f32[1,768,32]{1,2,0:T(8,128)} %get-tuple-element.43), kind=kOutput, calls=%fused_computation | convolution fusion | flops 227106816 | bytes 7274496 | tf_op jit(solution)/shard_map/mik,mjk->mij/dot_general | solution.py:89
  268.7 2.6 bitcast_subtract_fusion.1
  271.3 0.8 fusion.76
  272.1 1.9 fusion.77
  274.0 0.7 copy.44
  274.9 0.8 convolution_divide_fusion.2
  275.6 22.5 %all_gather.6 = bf16[2,192,768]{1,0,2:T(2,128)(2,1)S(1)} all-gather(bf16[2,192,48]{1,0,2:T(2,128)(2,1)} %copy.44), channel_id=1, replica_groups=mesh['shard'=16,'tensor'=4,'section'=2] {'shard'}, dimensions={2}, use_global_device_ids=true | all-gather | bytes 626688 | tf_op jit(solution)/shard_map/all_gather | solution.py:107
  298.2 2.0 copy.45
  300.1 1.7 copy.48
  301.8 1.7 copy.46
  303.5 1.7 copy.47
  305.2 1.8 convolution_bitcast_fusion
  307.0 0.9 fusion.13
  308.0 0.9 fusion.96
  309.1 0.2 fusion.12
  309.6 0.2 fusion.11
  309.8 0.2 convolution_divide_fusion
  310.0 1.0 fusion.31
  311.0 1.9 all-gather.2.cloned.1.call-done
  312.9 2.4 copy.49
  (83 shorter events, 5.0 us)
Async XLA Ops:
  7.2 13.0 %copy-start = (f32[2,768,32]{1,2,0:T(8,128)S(1)}, f32[2,768,32]{1,2,0:T(8,128)}, u32[]{:S(2)}) copy-start(f32[2,768,32]{1,2,0:T(8,128)} %param.20) | copy-start | bytes 589828
  7.2 3.3 %copy-start.5 = (f32[1,1,768,768]{3,2,1,0:T(8,128)S(1)}, f32[1,1,768,768]{3,2,1,0:T(8,128)}, u32[]{:S(2)}) copy-start(f32[1,1,768,768]{3,2,1,0:T(8,128)} %param.19) | copy-start | bytes 7077892
  7.2 95.1 %all-reduce.6.cloned.1.call-start = ((), (), s32[]{:S(2)}) async-start(), calls=%async_computation | async-start | bytes 196608 | tf_op jit(solution)/shard_map/psum | solution.py:67
  12.4 2.7 copy-start.11
  15.1 2.3 copy-start.16
  17.3 238.1 %all-reduce.8.cloned.1.call-start = ((), (), s32[]{:S(2)}) async-start(), calls=%async_computation.2 | async-start | bytes 589824 | tf_op jit(solution)/shard_map/psum | solution.py:77
  17.4 4.0 %copy-start.17 = (f32[1,1,192]{2,1,0:T(1,128)S(1)}, f32[1,1,192]{2,1,0:T(1,128)}, u32[]{:S(2)}) copy-start(f32[1,1,192]{2,1,0:T(1,128)} %param.26) | copy-start | bytes 2308
  19.2 1.0 copy-start.1
  102.3 24.4 %copy-start.7 = (f32[768,32]{0,1:T(8,128)S(1)}, f32[768,32]{0,1:T(8,128)}, u32[]{:S(2)}) copy-start(f32[768,32]{0,1:T(8,128)} %all-reduce.6.cloned.1.call-done) | copy-start | bytes 294916
  124.1 6.4 %copy-start.2 = (f32[1,2,192,768]{3,2,1,0:T(8,128)S(1)}, f32[1,2,192,768]{3,2,1,0:T(8,128)}, u32[]{:S(2)}) copy-start(f32[1,2,192,768]{3,2,1,0:T(8,128)} %copy-done.1) | copy-start | bytes 3538948
  127.0 5.2 %copy-start.18 = (f32[1,192]{1,0:T(1,128)S(1)}, f32[1,192]{1,0:T(1,128)}, u32[]{:S(2)}) copy-start(f32[1,192]{1,0:T(1,128)} %param.29) | copy-start | bytes 2308
  127.0 5.2 %copy-start.19 = (f32[1,192]{1,0:T(1,128)S(1)}, f32[1,192]{1,0:T(1,128)}, u32[]{:S(2)}) copy-start(f32[1,192]{1,0:T(1,128)} %param.28) | copy-start | bytes 2308
  127.0 5.8 %copy-start.12 = (f32[2,192,48]{1,2,0:T(8,128)S(1)}, f32[2,192,48]{1,2,0:T(8,128)}, u32[]{:S(2)}) copy-start(f32[2,192,48]{1,2,0:T(8,128)} %param.22) | copy-start | bytes 221188
  127.0 5.9 %copy-start.13 = (f32[2,192,48]{1,2,0:T(8,128)S(1)}, f32[2,192,48]{1,2,0:T(8,128)}, u32[]{:S(2)}) copy-start(f32[2,192,48]{1,2,0:T(8,128)} %param.24) | copy-start | bytes 221188
  127.0 6.0 %copy-start.14 = (f32[3,32]{1,0:T(4,128)S(1)}, f32[3,32]{1,0:T(4,128)}, u32[]{:S(2)}) copy-start(f32[3,32]{1,0:T(4,128)} %param.31) | copy-start | bytes 1156
  127.1 6.0 %copy-start.15 = (f32[3,32]{1,0:T(4,128)S(1)}, f32[3,32]{1,0:T(4,128)}, u32[]{:S(2)}) copy-start(f32[3,32]{1,0:T(4,128)} %param.30) | copy-start | bytes 1156
  132.0 181.0 %all-gather.2.cloned.1.call-start = ((), (), s32[]{:S(2)}) async-start(), calls=%async_computation.1 | async-start | bytes 1253376 | tf_op jit(solution)/shard_map/all_gather | solution.py:108
  264.2 4.5 %copy-start.3 = (f32[1,2,192,768]{3,2,1,0:T(8,128)S(1)}, f32[1,2,192,768]{3,2,1,0:T(8,128)}, u32[]{:S(2)}) copy-start(f32[1,2,192,768]{3,2,1,0:T(8,128)} %copy-done.1) | copy-start | bytes 3538948
  264.2 4.5 %copy-start.6 = (f32[2,768,32]{1,2,0:T(8,128)S(1)}, f32[2,768,32]{1,2,0:T(8,128)}, u32[]{:S(2)}) copy-start(f32[2,768,32]{1,2,0:T(8,128)} %get-tuple-element.42) | copy-start | bytes 589828
  268.7 2.6 copy-start.9
  268.7 2.6 copy-start.10
  271.3 26.9 %copy-start.4 = (f32[1,1,768,768]{2,3,1,0:T(8,128)S(1)}, f32[1,1,768,768]{2,3,1,0:T(8,128)}, u32[]{:S(2)}) copy-start(f32[1,1,768,768]{2,3,1,0:T(8,128)} %get-tuple-element.65) | copy-start | bytes 7077892
  300.1 8.8 %copy-start.8 = (f32[2,32,32]{2,1,0:T(8,128)S(1)}, f32[2,32,32]{2,1,0:T(8,128)}, u32[]{:S(2)}) copy-start(f32[2,32,32]{2,1,0:T(8,128)} %fusion.93) | copy-start | bytes 24580
  300.1 9.6 %copy-start.20 = (f32[2]{0:T(128)S(1)}, f32[2]{0:T(128)}, u32[]{:S(2)}) copy-start(f32[2]{0:T(128)} %get-tuple-element.59) | copy-start | bytes 28
Sparse Core Ops, SparseCore 0:
  17.5 84.7 all-reduce.5
  132.1 123.3 all-reduce.7
  272.2 40.6 all-gather.1
where the time goes:
time: 322 us
  waiting for transfers between devices  128 us (40%)
  blocking collectives  117 us (36%)
  matrix products  35.2 us (11%)
  local copies, waits for them, and re-layouts  16.6 us (5%)
  between operations  15.8 us (5%)
  other arithmetic  9.61 us (3%)
    psum x1, waiting for transfers between devices, per_device(): lax.psum((right_terms(attention_merged, attention_ortho), right_terms(fee...  122 us
    psum x1, blocking collectives, per_device(): lax.psum((attention_part, feedforward_part), 'shard')  76.9 us
    all_gather x1, blocking collectives, per_device(): lax.all_gather(attention_master_new.astype(jnp.bfloat16), 'shard', axis=2...  22.5 us
    psum x1, blocking collectives, per_device(): lax.psum((row_gram(attention_power), row_gram(feedforward_power)), 'tensor')  17.4 us
    unnamed x52, local copies, waits for them, and re-layouts  15.9 us
  transfers between devices with their start and end apart: 3, of which 3 were waited for; matrix products, arithmetic and copies ran while one was open for 6% of the time, Pallas kernels for 0%

commit v1 on v0

--- a/solution.py
+++ b/solution.py
@@ -7,6 +7,20 @@
 exact_mode = lax.Precision.HIGHEST
 learn_rate = 0.05
 decay_rate = 0.9
+
+
+def follow_spots(tile_in, a_name, d0):
+    axis_n = lax.axis_size(a_name)
+    shelf = tuple(((ix, (ix + 1) % axis_n) for ix in range(axis_n)))
+    column = tuple(((ix, (ix - 1) % axis_n) for ix in range(axis_n)))
+    val2, b_now = ([tile_in], [tile_in])
+    for _ in range(axis_n // 2):
+        val2.append(lax.ppermute(val2[-1], a_name, shelf))
+    for _ in [*range((axis_n - 1) // 2)]:
+        b_now.append(lax.ppermute(b_now[-1], a_name, column))
+    tall = jnp.concatenate([*val2[::-1], *b_now[1:]], axis=d0)
+    all_rows = jnp.roll(tall, (lax.axis_index(a_name) - axis_n // 2) * tile_in.shape[d0], d0)
+    return all_rows
 
 
 def inverse_root(gram_matrix):
@@ -104,7 +118,7 @@
     attention_master_new = attention_base - learn_rate * attention_slice
     feedforward_master_new = feedforward_base - learn_rate * feedforward_slice
     attention_fresh, feedforward_fresh = (
-        lax.all_gather(attention_master_new.astype(jnp.bfloat16), "shard", axis=2, tiled=True),
+        follow_spots(attention_master_new.astype(jnp.bfloat16), "shard", 2),
         lax.all_gather(feedforward_master_new.astype(jnp.bfloat16), "shard", axis=2, tiled=True),
     )
     gain_total, bias_total = lax.psum((gain_grads[0], bias_grads[0]), "shard")

time: 322 us -> 355 us (1.10)
  starting transfers between devices: 0.3 us -> 35.4 us
  blocking collectives: 117 us -> 94.2 us
  waiting for transfers between devices: 128 us -> 146 us
  local copies, waits for them, and re-layouts: 16.6 us -> 20.4 us
    ppermute x0 -> x15, starting transfers between devices: none -> 35.3 us  [the longest x7 35.2 us: follow_spots(): b_now.append(lax.ppermute(b_now[-1], a_name, column))]
    all_gather x1 -> x0, blocking collectives: 22.5 us -> none  [per_device(): lax.all_gather(attention_master_new.astype(jnp.bfloat16), 'shard', axis=2...]
    ppermute x0 -> x15, waiting for transfers between devices: none -> 21.1 us  [the longest x8 21 us: follow_spots(): val2.append(lax.ppermute(val2[-1], a_name, shelf))]
    concatenate x0 -> x1, local copies, waits for them, and re-layouts: none -> 5.09 us  [follow_spots(): jnp.roll(tall, (lax.axis_index(a_name) - axis_n // 2) * tile_in.shape[d0]...]
    unnamed x52 -> x67, local copies, waits for them, and re-layouts: 15.9 us -> 14.2 us
  transfers between devices with their start and end apart: 3 -> 18, of which waited for: 3 -> 10; matrix products, arithmetic and copies ran while one was open for 6% -> 7% of each run, Pallas kernels for 0% -> 0%
where the time goes in v1:
time: 355 us; the launch traced here: 354 us
  waiting for transfers between devices  146 us (41%)
  blocking collectives  94.2 us (27%)
  starting transfers between devices  35.4 us (10%)
  matrix products  34.9 us (10%)
  local copies, waits for them, and re-layouts  20.4 us (6%)
  between operations  15.8 us (4%)
  other arithmetic  7.82 us (2%)
    psum x1, waiting for transfers between devices, per_device(): lax.psum((right_terms(attention_merged, attention_ortho), right_terms(fee...  121 us
    psum x1, blocking collectives, per_device(): lax.psum((attention_part, feedforward_part), 'shard')  76.9 us
    ppermute x7, starting transfers between devices, follow_spots(): b_now.append(lax.ppermute(b_now[-1], a_name, column))  35.2 us
    ppermute x8, waiting for transfers between devices, follow_spots(): val2.append(lax.ppermute(val2[-1], a_name, shelf))  21 us
    psum x1, blocking collectives, per_device(): lax.psum((row_gram(attention_power), row_gram(feedforward_power)), 'tensor')  17.3 us
    unnamed x67, local copies, waits for them, and re-layouts  14.2 us
  transfers between devices with their start and end apart: 18, of which 10 were waited for; matrix products, arithmetic and copies ran while one was open for 7% of the time, Pallas kernels for 0%

profile of v1, /device:TPU:0, one launch (start us, length us, event | category | flops | bytes accessed | tf_op | source)
XLA Modules:
  0.0 354.1 jit_solution(261750418369688521)
XLA Ops:
  7.3 3.2 copy.30
  10.5 2.0 copy.31
  12.4 2.7 add.81
  15.2 2.2 fusion.2
  17.4 1.8 add.79
  19.2 1.0 copy-done.1
  20.2 1.2 fusion.6
  21.5 76.9 %all-reduce.1 = (f32[2,192,32]{1,2,0:T(8,128)S(1)}, f32[1,192]{1,0:T(1,128)S(1)}, f32[3,32]{1,0:T(4,128)S(1)}) all-reduce(f32[2,192,32]{1,2,0:T(8,128)S(1)} %fusion.6, f32[1,192]{1,0:T(1,128)S(1)} %bitcast.162, f32[3,32]{1,0:T(4,128)S(1)} %bitcast.161), channel_id=1, replica_groups=mesh['shard'=16,'tensor'=4,'section'=2] {'shard'}, use_global_device_ids=true, to_apply=%region_0.0 | all-reduce | flops 12576 | bytes 100608 | tf_op jit(solution)/shard_map/psum | solution.py:81
  98.3 0.2 fusion.78
  98.6 3.7 %all-reduce.6.cloned.1.call-done = f32[768,32]{0,1:T(8,128)} async-done(((f32[768,32]{0,1:T(8,128)}), f32[768,32]{0,1:T(8,128)}) %all-reduce.6.cloned.1.call-update) | async-done | bytes 98320 | tf_op jit(solution)/shard_map/psum | solution.py:81
  102.3 1.2 convolution_bitcast_fusion.1
  103.5 17.3 %all-reduce.2 = (f32[2,32,32]{2,1,0:T(8,128)S(1)}, f32[1,32,32]{2,1,0:T(8,128)S(1)}) all-reduce(f32[2,32,32]{2,1,0:T(8,128)S(1)} %fusion.78, f32[1,32,32]{2,1,0:T(8,128)S(1)} %convolution_bitcast_fusion.1), channel_id=1, replica_groups=mesh['shard'=16,'tensor'=4,'section'=2] {'tensor'}, use_global_device_ids=true, to_apply=%region_1.0 | all-reduce | flops 3072 | bytes 24576 | tf_op jit(solution)/shard_map/psum | solution.py:82
  120.9 0.6 multiply_reduce_fusion.3
  124.1 0.3 fusion.20
  124.4 0.2 fusion.66
  126.5 0.2 convolution_divide_fusion.1
  126.7 0.2 fusion.85
  127.2 0.3 fusion.92
  127.5 2.8 fusion.8
  130.4 1.4 fusion.4
  132.0 0.6 multiply_subtract_fusion.2
  132.5 0.8 copy.32
  133.3 0.8 copy.34
  134.1 0.6 multiply_subtract_fusion.1
  134.7 120.6 %all-reduce.8.cloned.1.call-done = (f32[2,768,32]{1,2,0:T(8,128)}, f32[1,768,32]{1,2,0:T(8,128)}) async-done(((f32[2,768,32]{1,2,0:T(8,128)}, f32[1,768,32]{1,2,0:T(8,128)}), (f32[2,768,32]{1,2,0:T(8,128)}, f32[1,768,32]{1,2,0:T(8,128)})) %all-reduce.8.cloned.1.call-update) | async-done | bytes 294928 | tf_op jit(solution)/shard_map/psum | solution.py:91
  255.3 1.8 multiply_reduce_fusion.2
  258.4 0.8 fusion.100
  259.2 0.7 fusion.99
  259.9 1.4 multiply_reduce_fusion
  261.4 0.5 fusion.75
  261.9 0.2 fusion.15
  262.2 0.2 fusion.67
  263.8 0.8 fusion.97
  264.5 0.8 fusion.98
  265.3 2.1 bitcast_subtract_fusion.1
  267.6 2.8 collective-permute-start.8
  270.4 3.5 bitcast_subtract_fusion
  274.0 0.8 fusion.76
  274.8 1.0 fusion.11
  275.8 1.0 convolution_divide_fusion
  276.8 0.9 fusion.23
  277.6 1.0 fusion.31
  279.0 5.4 %collective-permute-start.9 = (bf16[2,192,48]{2,1,0:T(8,128)(2,1)S(1)}, bf16[2,192,48]{2,1,0:T(8,128)(2,1)S(1)}, u32[]{:S(2)}, u32[]{:S(2)}) collective-permute-start(bf16[2,192,48]{2,1,0:T(8,128)(2,1)S(1)} %collective-permute-done.8), channel_id=1, source_target_pairs={{0,120},{8,0},{16,8},{24,16},{32,24},{40,32},{48,40},{56,48},{64,5... | collective-permute-start | bytes 110600 | tf_op jit(solution)/shard_map/ppermute | solution.py:20
  284.4 2.6 collective-permute-done.1
  287.2 5.4 %collective-permute-start.10 = (bf16[2,192,48]{2,1,0:T(8,128)(2,1)S(1)}, bf16[2,192,48]{2,1,0:T(8,128)(2,1)S(1)}, u32[]{:S(2)}, u32[]{:S(2)}) collective-permute-start(bf16[2,192,48]{2,1,0:T(8,128)(2,1)S(1)} %collective-permute-done.9), channel_id=1, source_target_pairs={{0,120},{8,0},{16,8},{24,16},{32,24},{40,32},{48,40},{56,48},{64,5... | collective-permute-start | bytes 110600 | tf_op jit(solution)/shard_map/ppermute | solution.py:20
  292.6 2.6 collective-permute-done.2
  295.3 5.4 %collective-permute-start.11 = (bf16[2,192,48]{2,1,0:T(8,128)(2,1)S(1)}, bf16[2,192,48]{2,1,0:T(8,128)(2,1)}, u32[]{:S(2)}, u32[]{:S(2)}) collective-permute-start(bf16[2,192,48]{2,1,0:T(8,128)(2,1)S(1)} %collective-permute-done.10), channel_id=1, source_target_pairs={{0,120},{8,0},{16,8},{24,16},{32,24},{40,32},{48,40},{56,48},{64,5... | collective-permute-start | bytes 110600 | tf_op jit(solution)/shard_map/ppermute | solution.py:20
  300.7 2.4 collective-permute-done.3
  303.3 0.5 copy-done.13
  303.8 5.0 %collective-permute-start.12 = (bf16[2,192,48]{2,1,0:T(8,128)(2,1)}, bf16[2,192,48]{2,1,0:T(8,128)(2,1)}, u32[]{:S(2)}, u32[]{:S(2)}) collective-permute-start(bf16[2,192,48]{2,1,0:T(8,128)(2,1)} %collective-permute-done.11), channel_id=1, source_target_pairs={{0,120},{8,0},{16,8},{24,16},{32,24},{40,32},{48,40},{56,48},{64,5... | collective-permute-start | bytes 110600 | tf_op jit(solution)/shard_map/ppermute | solution.py:20
  308.8 4.4 %collective-permute-done.4 = bf16[2,192,48]{2,1,0:T(8,128)(2,1)} collective-permute-done((bf16[2,192,48]{2,1,0:T(8,128)(2,1)S(1)}, bf16[2,192,48]{2,1,0:T(8,128)(2,1)}, u32[]{:S(2)}, u32[]{:S(2)}) %collective-permute-start.4) | collective-permute-done | bytes 36896 | tf_op jit(solution)/shard_map/ppermute | solution.py:18
  313.5 5.8 %collective-permute-start.13 = (bf16[2,192,48]{2,1,0:T(8,128)(2,1)}, bf16[2,192,48]{2,1,0:T(8,128)(2,1)}, u32[]{:S(2)}, u32[]{:S(2)}) collective-permute-start(bf16[2,192,48]{2,1,0:T(8,128)(2,1)} %collective-permute-done.12), channel_id=1, source_target_pairs={{0,120},{8,0},{16,8},{24,16},{32,24},{40,32},{48,40},{56,48},{64,5... | collective-permute-start | bytes 110600 | tf_op jit(solution)/shard_map/ppermute | solution.py:20
  319.3 3.2 collective-permute-done.5
  322.5 0.9 convolution_divide_fusion.2
  323.4 5.4 %collective-permute-start.14 = (bf16[2,192,48]{2,1,0:T(8,128)(2,1)}, bf16[2,192,48]{2,1,0:T(8,128)(2,1)}, u32[]{:S(2)}, u32[]{:S(2)}) collective-permute-start(bf16[2,192,48]{2,1,0:T(8,128)(2,1)} %collective-permute-done.13), channel_id=1, source_target_pairs={{0,120},{8,0},{16,8},{24,16},{32,24},{40,32},{48,40},{56,48},{64,5... | collective-permute-start | bytes 110600 | tf_op jit(solution)/shard_map/ppermute | solution.py:20
  328.8 2.0 collective-permute-done.6
  330.8 0.9 convolution_bitcast_fusion
  331.7 0.8 copy.37
  332.4 0.8 copy.36
  333.2 1.9 copy.35
  335.1 3.9 %collective-permute-done.7 = bf16[2,192,48]{2,1,0:T(8,128)(2,1)} collective-permute-done((bf16[2,192,48]{2,1,0:T(8,128)(2,1)}, bf16[2,192,48]{2,1,0:T(8,128)(2,1)}, u32[]{:S(2)}, u32[]{:S(2)}) %collective-permute-start.7) | collective-permute-done | bytes 36896 | tf_op jit(solution)/shard_map/ppermute | solution.py:18
  339.0 5.1 %concatenate.6 = bf16[2,192,1536]{2,1,0:T(8,128)(2,1)S(1)} concatenate(bf16[2,192,48]{2,1,0:T(8,128)(2,1)} %collective-permute-done.7, bf16[2,192,48]{2,1,0:T(8,128)(2,1)} %collective-permute-done.6, bf16[2,192,48]{2,1,0:T(8,128)(2,1)} %collective-permute-done.5, bf16[2,192,48]{2,1,0:T(8,128)(2,1)} %collective-permute-done.4, bf16[2,192,48]{2,1,0:T(8,128)(2,1)S(1)} %copy-done.14, ...), dimensions={2} | concatenate | bytes 2359296 | tf_op jit(solution)/shard_map/jit(_roll_dynamic)/concatenate | solution.py:22
  344.1 1.1 constant_dynamic-slice_fusion
  345.2 2.4 copy.38
  (128 shorter events, 7.4 us)
Async XLA Ops:
  7.2 13.0 %copy-start = (f32[2,768,32]{1,2,0:T(8,128)S(1)}, f32[2,768,32]{1,2,0:T(8,128)}, u32[]{:S(2)}) copy-start(f32[2,768,32]{1,2,0:T(8,128)} %param.20) | copy-start | bytes 589828
  7.2 3.3 copy-start.5
  7.2 95.1 %all-reduce.6.cloned.1.call-start = ((), (), s32[]{:S(2)}) async-start(), calls=%async_computation | async-start | bytes 196608 | tf_op jit(solution)/shard_map/psum | solution.py:81
  12.4 2.7 copy-start.19
  15.1 2.3 copy-start.25
  17.4 238.0 %all-reduce.8.cloned.1.call-start = ((), (), s32[]{:S(2)}) async-start(), calls=%async_computation.2 | async-start | bytes 589824 | tf_op jit(solution)/shard_map/psum | solution.py:91
  19.2 1.0 copy-start.1
  20.2 1.2 copy-start.26
  122.3 4.9 %copy-start.8 = (f32[768,32]{0,1:T(8,128)S(1)}, f32[768,32]{0,1:T(8,128)}, u32[]{:S(2)}) copy-start(f32[768,32]{0,1:T(8,128)} %all-reduce.6.cloned.1.call-done) | copy-start | bytes 294916
  127.5 2.9 copy-start.2
  130.4 1.5 copy-start.27
  130.4 1.5 copy-start.28
  130.4 2.1 copy-start.20
  130.4 2.9 copy-start.21
  130.4 3.7 %copy-start.23 = (f32[3,32]{1,0:T(4,128)S(1)}, f32[3,32]{1,0:T(4,128)}, u32[]{:S(2)}) copy-start(f32[3,32]{1,0:T(4,128)} %param.31) | copy-start | bytes 1156
  130.4 3.7 %copy-start.24 = (f32[3,32]{1,0:T(4,128)S(1)}, f32[3,32]{1,0:T(4,128)}, u32[]{:S(2)}) copy-start(f32[3,32]{1,0:T(4,128)} %param.30) | copy-start | bytes 1156
  131.9 213.3 %all-gather.2.cloned.1.call-start = ((), (), s32[]{:S(2)}) async-start(), calls=%async_computation.1 | async-start | bytes 1253376 | tf_op jit(solution)/shard_map/all_gather | solution.py:122
  255.3 10.0 %copy-start.6 = (f32[2,768,32]{1,2,0:T(8,128)S(1)}, f32[2,768,32]{1,2,0:T(8,128)}, u32[]{:S(2)}) copy-start(f32[2,768,32]{1,2,0:T(8,128)} %get-tuple-element.28) | copy-start | bytes 589828
  257.8 7.5 %copy-start.3 = (f32[1,2,192,768]{3,2,1,0:T(8,128)S(1)}, f32[1,2,192,768]{3,2,1,0:T(8,128)}, u32[]{:S(2)}) copy-start(f32[1,2,192,768]{3,2,1,0:T(8,128)} %copy-done.1) | copy-start | bytes 3538948
  265.3 2.2 copy-start.9
  265.3 2.2 copy-start.10
  265.3 5.1 %copy-start.7 = (f32[1,768,32]{1,2,0:T(8,128)S(1)}, f32[1,768,32]{1,2,0:T(8,128)}, u32[]{:S(2)}) copy-start(f32[1,768,32]{1,2,0:T(8,128)} %get-tuple-element.29) | copy-start | bytes 294916
  267.6 6.3 %copy-start.17 = (f32[1,768,48]{1,2,0:T(8,128)S(1)}, f32[1,768,48]{1,2,0:T(8,128)}, u32[]{:S(2)}) copy-start(f32[1,768,48]{1,2,0:T(8,128)} %param.25) | copy-start | bytes 442372
  267.6 6.3 %copy-start.18 = (f32[1,768,48]{1,2,0:T(8,128)S(1)}, f32[1,768,48]{1,2,0:T(8,128)}, u32[]{:S(2)}) copy-start(f32[1,768,48]{1,2,0:T(8,128)} %param.23) | copy-start | bytes 442372
  267.6 11.4 %collective-permute-start.8 = (bf16[2,192,48]{2,1,0:T(8,128)(2,1)S(1)}, bf16[2,192,48]{2,1,0:T(8,128)(2,1)S(1)}, u32[]{:S(2)}, u32[]{:S(2)}) collective-permute-start(bf16[2,192,48]{2,1,0:T(8,128)(2,1)S(1)} %get-tuple-element.41), channel_id=1, source_target_pairs={{0,120},{8,0},{16,8},{24,16},{32,24},{40,32},{48,40},{56,48},{64,5... | collective-permute-start | bytes 110600 | tf_op jit(solution)/shard_map/ppermute | solution.py:20
  270.4 8.4 %collective-permute-start = (bf16[2,192,48]{2,1,0:T(8,128)(2,1)S(1)}, bf16[2,192,48]{2,1,0:T(8,128)(2,1)}, u32[]{:S(2)}, u32[]{:S(2)}) collective-permute-start(bf16[2,192,48]{2,1,0:T(8,128)(2,1)S(1)} %get-tuple-element.41), channel_id=1, source_target_pairs={{0,8},{8,16},{16,24},{24,32},{32,40},{40,48},{48,56},{56,64},{64,7... | collective-permute-start | bytes 110600 | tf_op jit(solution)/shard_map/ppermute | solution.py:18
  273.9 4.7 %copy-start.16 = (f32[32,32]{1,0:T(8,128)S(1)}, f32[32,32]{1,0:T(8,128)}, u32[]{:S(2)}) copy-start(f32[32,32]{1,0:T(8,128)} %fusion.100) | copy-start | bytes 12292
  273.9 4.9 %copy-start.15 = (f32[32,32]{1,0:T(8,128)S(1)}, f32[32,32]{1,0:T(8,128)}, u32[]{:S(2)}) copy-start(f32[32,32]{1,0:T(8,128)} %fusion.99) | copy-start | bytes 12292
  273.9 59.2 %copy-start.4 = (f32[1,1,768,768]{2,3,1,0:T(8,128)S(1)}, f32[1,1,768,768]{2,3,1,0:T(8,128)}, u32[]{:S(2)}) copy-start(f32[1,1,768,768]{2,3,1,0:T(8,128)} %get-tuple-element.51) | copy-start | bytes 7077892
  278.8 8.2 %collective-permute-start.1 = (bf16[2,192,48]{2,1,0:T(8,128)(2,1)}, bf16[2,192,48]{2,1,0:T(8,128)(2,1)S(1)}, u32[]{:S(2)}, u32[]{:S(2)}) collective-permute-start(bf16[2,192,48]{2,1,0:T(8,128)(2,1)} %collective-permute-done), channel_id=1, source_target_pairs={{0,8},{8,16},{16,24},{24,32},{32,40},{40,48},{48,56},{56,64},{64,7... | collective-permute-start | bytes 110600 | tf_op jit(solution)/shard_map/ppermute | solution.py:18
  279.0 8.1 %collective-permute-start.9 = (bf16[2,192,48]{2,1,0:T(8,128)(2,1)S(1)}, bf16[2,192,48]{2,1,0:T(8,128)(2,1)S(1)}, u32[]{:S(2)}, u32[]{:S(2)}) collective-permute-start(bf16[2,192,48]{2,1,0:T(8,128)(2,1)S(1)} %collective-permute-done.8), channel_id=1, source_target_pairs={{0,120},{8,0},{16,8},{24,16},{32,24},{40,32},{48,40},{56,48},{64,5... | collective-permute-start | bytes 110600 | tf_op jit(solution)/shard_map/ppermute | solution.py:20
  287.0 8.1 %collective-permute-start.2 = (bf16[2,192,48]{2,1,0:T(8,128)(2,1)S(1)}, bf16[2,192,48]{2,1,0:T(8,128)(2,1)S(1)}, u32[]{:S(2)}, u32[]{:S(2)}) collective-permute-start(bf16[2,192,48]{2,1,0:T(8,128)(2,1)S(1)} %collective-permute-done.1), channel_id=1, source_target_pairs={{0,8},{8,16},{16,24},{24,32},{32,40},{40,48},{48,56},{56,64},{64,7... | collective-permute-start | bytes 110600 | tf_op jit(solution)/shard_map/ppermute | solution.py:18
  287.2 8.1 %collective-permute-start.10 = (bf16[2,192,48]{2,1,0:T(8,128)(2,1)S(1)}, bf16[2,192,48]{2,1,0:T(8,128)(2,1)S(1)}, u32[]{:S(2)}, u32[]{:S(2)}) collective-permute-start(bf16[2,192,48]{2,1,0:T(8,128)(2,1)S(1)} %collective-permute-done.9), channel_id=1, source_target_pairs={{0,120},{8,0},{16,8},{24,16},{32,24},{40,32},{48,40},{56,48},{64,5... | collective-permute-start | bytes 110600 | tf_op jit(solution)/shard_map/ppermute | solution.py:20
  295.1 8.0 %collective-permute-start.3 = (bf16[2,192,48]{2,1,0:T(8,128)(2,1)S(1)}, bf16[2,192,48]{2,1,0:T(8,128)(2,1)S(1)}, u32[]{:S(2)}, u32[]{:S(2)}) collective-permute-start(bf16[2,192,48]{2,1,0:T(8,128)(2,1)S(1)} %collective-permute-done.2), channel_id=1, source_target_pairs={{0,8},{8,16},{16,24},{24,32},{32,40},{40,48},{48,56},{56,64},{64,7... | collective-permute-start | bytes 110600 | tf_op jit(solution)/shard_map/ppermute | solution.py:18
  295.3 17.9 %copy-start.22 = (f32[32,32]{1,0:T(8,128)}, f32[32,32]{1,0:T(8,128)S(1)}, u32[]{:S(2)}) copy-start(f32[32,32]{1,0:T(8,128)S(1)} %fusion.103) | copy-start | bytes 12292
  295.3 7.8 %copy-start.11 = (bf16[2,192,48]{2,1,0:T(8,128)(2,1)}, bf16[2,192,48]{2,1,0:T(8,128)(2,1)S(1)}, u32[]{:S(2)}) copy-start(bf16[2,192,48]{2,1,0:T(8,128)(2,1)S(1)} %collective-permute-done.10) | copy-start | bytes 110596
  295.3 7.9 %collective-permute-start.11 = (bf16[2,192,48]{2,1,0:T(8,128)(2,1)S(1)}, bf16[2,192,48]{2,1,0:T(8,128)(2,1)}, u32[]{:S(2)}, u32[]{:S(2)}) collective-permute-start(bf16[2,192,48]{2,1,0:T(8,128)(2,1)S(1)} %collective-permute-done.10), channel_id=1, source_target_pairs={{0,120},{8,0},{16,8},{24,16},{32,24},{40,32},{48,40},{56,48},{64,5... | collective-permute-start | bytes 110600 | tf_op jit(solution)/shard_map/ppermute | solution.py:20
  303.1 0.6 copy-start.13
  303.1 10.1 %collective-permute-start.4 = (bf16[2,192,48]{2,1,0:T(8,128)(2,1)S(1)}, bf16[2,192,48]{2,1,0:T(8,128)(2,1)}, u32[]{:S(2)}, u32[]{:S(2)}) collective-permute-start(bf16[2,192,48]{2,1,0:T(8,128)(2,1)S(1)} %collective-permute-done.3), channel_id=1, source_target_pairs={{0,8},{8,16},{16,24},{24,32},{32,40},{40,48},{48,56},{56,64},{64,7... | collective-permute-start | bytes 110600 | tf_op jit(solution)/shard_map/ppermute | solution.py:18
  303.8 9.7 %collective-permute-start.12 = (bf16[2,192,48]{2,1,0:T(8,128)(2,1)}, bf16[2,192,48]{2,1,0:T(8,128)(2,1)}, u32[]{:S(2)}, u32[]{:S(2)}) collective-permute-start(bf16[2,192,48]{2,1,0:T(8,128)(2,1)} %collective-permute-done.11), channel_id=1, source_target_pairs={{0,120},{8,0},{16,8},{24,16},{32,24},{40,32},{48,40},{56,48},{64,5... | collective-permute-start | bytes 110600 | tf_op jit(solution)/shard_map/ppermute | solution.py:20
  313.2 9.3 %collective-permute-start.5 = (bf16[2,192,48]{2,1,0:T(8,128)(2,1)}, bf16[2,192,48]{2,1,0:T(8,128)(2,1)}, u32[]{:S(2)}, u32[]{:S(2)}) collective-permute-start(bf16[2,192,48]{2,1,0:T(8,128)(2,1)} %collective-permute-done.4), channel_id=1, source_target_pairs={{0,8},{8,16},{16,24},{24,32},{32,40},{40,48},{48,56},{56,64},{64,7... | collective-permute-start | bytes 110600 | tf_op jit(solution)/shard_map/ppermute | solution.py:18
  313.5 9.9 %collective-permute-start.13 = (bf16[2,192,48]{2,1,0:T(8,128)(2,1)}, bf16[2,192,48]{2,1,0:T(8,128)(2,1)}, u32[]{:S(2)}, u32[]{:S(2)}) collective-permute-start(bf16[2,192,48]{2,1,0:T(8,128)(2,1)} %collective-permute-done.12), channel_id=1, source_target_pairs={{0,120},{8,0},{16,8},{24,16},{32,24},{40,32},{48,40},{56,48},{64,5... | collective-permute-start | bytes 110600 | tf_op jit(solution)/shard_map/ppermute | solution.py:20
  322.5 8.3 %collective-permute-start.6 = (bf16[2,192,48]{2,1,0:T(8,128)(2,1)}, bf16[2,192,48]{2,1,0:T(8,128)(2,1)}, u32[]{:S(2)}, u32[]{:S(2)}) collective-permute-start(bf16[2,192,48]{2,1,0:T(8,128)(2,1)} %collective-permute-done.5), channel_id=1, source_target_pairs={{0,8},{8,16},{16,24},{24,32},{32,40},{40,48},{48,56},{56,64},{64,7... | collective-permute-start | bytes 110600 | tf_op jit(solution)/shard_map/ppermute | solution.py:18
  323.4 11.8 %collective-permute-start.14 = (bf16[2,192,48]{2,1,0:T(8,128)(2,1)}, bf16[2,192,48]{2,1,0:T(8,128)(2,1)}, u32[]{:S(2)}, u32[]{:S(2)}) collective-permute-start(bf16[2,192,48]{2,1,0:T(8,128)(2,1)} %collective-permute-done.13), channel_id=1, source_target_pairs={{0,120},{8,0},{16,8},{24,16},{32,24},{40,32},{48,40},{56,48},{64,5... | collective-permute-start | bytes 110600 | tf_op jit(solution)/shard_map/ppermute | solution.py:20
  330.8 8.3 %collective-permute-start.7 = (bf16[2,192,48]{2,1,0:T(8,128)(2,1)}, bf16[2,192,48]{2,1,0:T(8,128)(2,1)}, u32[]{:S(2)}, u32[]{:S(2)}) collective-permute-start(bf16[2,192,48]{2,1,0:T(8,128)(2,1)} %collective-permute-done.6), channel_id=1, source_target_pairs={{0,8},{8,16},{16,24},{24,32},{32,40},{40,48},{48,56},{56,64},{64,7... | collective-permute-start | bytes 110600 | tf_op jit(solution)/shard_map/ppermute | solution.py:18
  333.2 5.8 %copy-start.12 = (bf16[2,192,48]{2,1,0:T(8,128)(2,1)S(1)}, bf16[2,192,48]{2,1,0:T(8,128)(2,1)}, u32[]{:S(2)}) copy-start(bf16[2,192,48]{2,1,0:T(8,128)(2,1)} %copy-done.11) | copy-start | bytes 110596
  333.2 5.8 %copy-start.14 = (bf16[2,192,48]{2,1,0:T(8,128)(2,1)S(1)}, bf16[2,192,48]{2,1,0:T(8,128)(2,1)}, u32[]{:S(2)}) copy-start(bf16[2,192,48]{2,1,0:T(8,128)(2,1)} %copy-done.13) | copy-start | bytes 110596
Sparse Core Ops, SparseCore 0:
  17.5 84.7 all-reduce.5
  132.0 123.2 all-reduce.7
  274.9 44.5 all-gather.1
